TPU v7x, 32 devices: a whole 2x2x4 slice. The times are simulated.
32 devices in a mesh: freq: 4 (over y, x), param: 8 (over z, core).
Axes of the slice: x: 2, y: 2, z: 4, core: 2. Of those that a mesh axis runs over, the one named last changes fastest.
Arguments:
- chain_state: float32 [32, 2048, 512], P('freq', 'param'), may hold values from -6 to 6
- second_moment: float32 [32, 2048, 512], P('freq', 'param'), may hold values from 0.25 to 2
- noise: float32 [2, 32, 2048, 512], P(None, 'freq', 'param'), may hold values from -6 to 6
- green: bfloat16 [2, 64, 2048, 512], P(None, 'freq', 'param'), may hold values from -0.125 to 0.125
- observed: float32 [64, 1024], P('freq'), may hold values from -6 to 6
- inv_noise: float32 [64, 512], P('freq'), may hold values from 0.3 to 3
- temper: float32 [32], P('freq'), may hold values from 0.2 to 1
Outputs:
- new_state: float32 [32, 2048, 512], P('freq', 'param')
- new_moment: float32 [32, 2048, 512], P('freq', 'param')
All inputs are finite; a program needn't handle non-finite values.
Results may differ from a plain program's by a relative error of at most 0.005.
Values may be sent and summed in bfloat16 or wider, within the bound.
A program may use at most 128 MiB of HBM per device.

v0:
```python
import math
import jax
import jax.numpy as jnp
from jax import lax
from jax.sharding import PartitionSpec as P

decay_rate = 0.9
step_length = 0.5


def spectral_table(time_len, freq_total):
    time_index = jnp.arange(time_len, dtype=jnp.int32)[:, None]
    wave_number = jnp.arange(freq_total, dtype=jnp.int32)[None, :] + 1
    phase_angle = (time_index * wave_number % time_len).astype(jnp.float32) * (
        2.0 * math.pi / time_len
    )
    columns_table = jnp.stack([jnp.cos(phase_angle), -jnp.sin(phase_angle)], axis=-1).reshape(
        time_len, 2 * freq_total
    )
    return (columns_table / math.sqrt(time_len)).astype(jnp.bfloat16)


def on_device(chain_state, second_moment, noise, green, observed, inv_noise, temper):
    chains_loc, slab_rows, time_len = chain_state.shape
    freq_loc = green.shape[1]
    freq_count = lax.axis_size("freq")
    freq_total = freq_loc * freq_count
    chains = chains_loc * freq_count
    forward_table = spectral_table(time_len, freq_total)
    inverse_table = forward_table.T
    green_re = green[0]
    green_im = green[1]
    upper_rows = jnp.concatenate([green_re, green_im], axis=2)
    lower_rows = jnp.concatenate([-green_im, green_re], axis=2)
    kernel = jnp.concatenate([upper_rows, lower_rows], axis=1)
    weights = jnp.concatenate([inv_noise, inv_noise], axis=1)
    temper_cols = temper[:, None, None]
    current = chain_state
    moment = second_moment
    for step_num in range(noise.shape[0]):
        low_state = current.astype(jnp.bfloat16)
        local_spec = jnp.dot(
            low_state.reshape(chains_loc * slab_rows, time_len),
            forward_table,
            preferred_element_type=jnp.float32,
        )
        local_spec = local_spec.astype(jnp.bfloat16).reshape(chains_loc, slab_rows, 2 * freq_total)
        spectrum = lax.all_to_all(local_spec, "freq", split_axis=2, concat_axis=0, tiled=True)
        mixed_spec = (
            spectrum.reshape(chains, slab_rows, freq_loc, 2)
            .transpose(2, 0, 3, 1)
            .reshape(freq_loc, chains, 2 * slab_rows)
        )
        partial_data = jnp.einsum(
            "fcq,fqs->fcs", mixed_spec, kernel, preferred_element_type=jnp.float32
        )
        predicted = lax.psum(partial_data.astype(jnp.bfloat16), "param").astype(jnp.float32)
        weighted = (weights[:, None, :] * (predicted - observed[:, None, :])).astype(jnp.bfloat16)
        adjoint = jnp.einsum(
            "fcs,fqs->fcq", weighted, kernel, preferred_element_type=jnp.float32
        ).astype(jnp.bfloat16)
        adjoint = (
            adjoint.reshape(freq_loc, chains, 2, slab_rows)
            .transpose(1, 3, 0, 2)
            .reshape(chains, slab_rows, 2 * freq_loc)
        )
        own_adjoint = lax.all_to_all(adjoint, "freq", split_axis=0, concat_axis=2, tiled=True)
        gradient = jnp.dot(
            own_adjoint.reshape(chains_loc * slab_rows, 2 * freq_total),
            inverse_table,
            preferred_element_type=jnp.float32,
        )
        gradient = gradient.reshape(chains_loc, slab_rows, time_len)
        drift_term = temper_cols * gradient + current
        moment = decay_rate * moment + (1.0 - decay_rate) * drift_term * drift_term
        precondition = lax.rsqrt(moment)
        current = (
            current
            - step_length * precondition * drift_term
            + math.sqrt(2.0 * step_length) * jnp.sqrt(precondition) * noise[step_num]
        )
    return (current, moment)


def solution(mesh):
    return jax.shard_map(
        on_device,
        mesh=mesh,
        in_specs=(
            P("freq", "param", None),
            P("freq", "param", None),
            P(None, "freq", "param", None),
            P(None, "freq", "param", None),
            P("freq", None),
            P("freq", None),
            P("freq"),
        ),
        out_specs=(P("freq", "param", None), P("freq", "param", None)),
        check_vma=False,
    )
```

profile of v0, /device:TPU:0, one launch (start us, length us, event | category | flops | bytes accessed | tf_op | source)
XLA Modules:
  0.0 238.1 jit_solution(13732761810308003860)
XLA Ops:
  7.2 0.6 fusion.19
  7.8 0.1 copy.56
  7.9 0.1 convert_element_type.81
  8.0 2.5 %convert_element_type.82 = bf16[8,256,512]{2,1,0:T(8,128)(2,1)S(1)} convert(f32[8,256,512]{2,1,0:T(8,128)} %param.7) | non-fusion elementwise | flops 1048576 | bytes 6291456 | tf_op jit(solution)/shard_map/convert_element_type | solution.py:41
  10.5 0.8 convolution_convert_fusion.1
  11.3 0.9 copy.86
  12.2 5.2 %all-to-all-start = ((bf16[8,256,128]{1,0,2:T(8,128)(2,1)}), bf16[8,256,128]{1,0,2:T(8,128)(2,1)S(1)}, u32[]{:S(2)}, u32[]{:S(2)}) async-start(bf16[8,256,128]{1,0,2:T(8,128)(2,1)} %bitcast.48), calls=%async_computation | async-start | bytes 1048576 | tf_op jit(solution)/shard_map/all_to_all | solution.py:48
  17.4 5.9 %slice_bitcast_fusion = (bf16[16,256,512]{2,1,0:T(8,128)(2,1)}, bf16[16,256,512]{2,1,0:T(8,128)(2,1)}) fusion(bf16[2,16,256,512]{3,2,1,0:T(8,128)(2,1)} %param.10), kind=kLoop, calls=%fused_computation.11 | loop fusion | bytes 16777216 | tf_op jit(solution)/shard_map/squeeze | solution.py:32
  23.3 4.4 %fusion.20 = bf16[16,256,512]{2,1,0:T(8,128)(2,1)} fusion(bf16[2,16,256,512]{3,2,1,0:T(8,128)(2,1)} %param.10), kind=kLoop, calls=%fused_computation.46 | loop fusion | flops 2097152 | bytes 8388608 | tf_op jit(solution)/shard_map/neg | solution.py:34
  27.8 0.0 copy-start.2
  27.8 0.0 copy-start.4
  27.8 8.4 %convolution_convert_fusion.3 = bf16[16,32,1024]{2,1,0:T(8,128)(2,1)} fusion(bf16[16,32,512]{2,1,0:T(8,128)(2,1)S(1)} %bitcast.98, bf16[16,256,512]{2,1,0:T(8,128)(2,1)} %get-tuple-element.7, bf16[16,256,512]{2,1,0:T(8,128)(2,1)} %fusion.20, bf16[16,256,512]{2,1,0:T(8,128)(2,1)} %get-tuple-element.6), kind=kOutput, calls=%fused_computation.18 | convolution fusion | flops 604504064 | bytes 14155776 | tf_op jit(solution)/shard_map/fcq,fqs->fcs/dot_general | solution.py:54
  36.3 0.0 all-reduce.3.cloned.1.call-update
  36.3 0.0 all-reduce.5.cloned.1.call-start
  36.4 61.1 %all-reduce.3.cloned.1.call-done = bf16[16,32,1024]{2,1,0:T(8,128)(2,1)} async-done(((bf16[16,32,1024]{2,1,0:T(8,128)(2,1)}), bf16[16,32,1024]{2,1,0:T(8,128)(2,1)}) %all-reduce.3.cloned.1.call-update) | async-done | bytes 1048592 | tf_op jit(solution)/shard_map/psum | solution.py:57
  97.5 8.7 %convolution_convert_fusion.5 = bf16[16,32,512]{2,1,0:T(8,128)(2,1)S(1)} fusion(bf16[16,32,1024]{2,1,0:T(8,128)(2,1)} %all-reduce.3.cloned.1.call-done, f32[16,1024]{1,0:T(8,128)S(1)} %copy-done.4, f32[16,1024]{1,0:T(8,128)S(1)} %pad_maximum_fusion, bf16[16,256,512]{2,1,0:T(8,128)(2,1)} %get-tuple-element.7, bf16[16,256,512]{2,1,0:T(8,128)(2,1)} %fusion.20, ...), kind=kOutput, calls=%fused_computation.20 | convolution fusion | flops 606339072 | bytes 14286848 | tf_op jit(solution)/shard_map/fcs,fqs->fcq/dot_general | solution.py:59
  106.2 0.0 copy-start
  106.3 0.1 copy.92
  106.3 0.3 copy.61
  106.6 10.8 %all_to_all.60 = bf16[32,256,32]{1,2,0:T(8,128)(2,1)S(1)} all-to-all(bf16[32,256,32]{1,2,0:T(8,128)(2,1)S(1)} %copy.61), channel_id=1, replica_groups=mesh['freq'=4,'param'=8] {'freq'}, dimensions={0} | all-to-all | bytes 1048576 | tf_op jit(solution)/shard_map/all_to_all | solution.py:67
  117.5 7.4 %fusion.22 = (bf16[8,256,512]{2,1,0:T(8,128)(2,1)S(1)}, f32[8,256,512]{2,1,0:T(8,128)}, f32[8,256,512]{2,1,0:T(8,128)}) fusion(f32[2,8,256,512]{3,2,1,0:T(8,128)} %param.9, f32[8,256,512]{2,1,0:T(8,128)S(1)} %copy-done, f32[8]{0:T(128)S(1)} %copy-done.3, f32[8,256,512]{2,1,0:T(8,128)} %param.8, bf16[8,256,128]{1,2,0:T(8,128)(2,1)S(1)} %bitcast.88, ...), kind=kOutput, calls=%fused_computation.47 | convolution fusion | flops 281018368 | bytes 23724064 | tf_op jit(solution)/shard_map/dot_general | solution.py:68
  124.8 0.7 convolution_convert_fusion
  125.5 0.4 copy.65
  125.9 9.5 %all_to_all.61 = bf16[8,256,128]{1,0,2:T(8,128)(2,1)S(1)} all-to-all(bf16[8,256,128]{1,0,2:T(8,128)(2,1)S(1)} %copy.65), channel_id=1, replica_groups=mesh['freq'=4,'param'=8] {'freq'}, dimensions={2} | all-to-all | bytes 1048576 | tf_op jit(solution)/shard_map/all_to_all | solution.py:48
  135.5 8.4 %convolution_convert_fusion.2 = bf16[16,32,1024]{2,1,0:T(8,128)(2,1)} fusion(bf16[16,32,512]{2,1,0:T(8,128)(2,1)S(1)} %bitcast.100, bf16[16,256,512]{2,1,0:T(8,128)(2,1)} %get-tuple-element.7, bf16[16,256,512]{2,1,0:T(8,128)(2,1)} %fusion.20, bf16[16,256,512]{2,1,0:T(8,128)(2,1)} %get-tuple-element.6), kind=kOutput, calls=%fused_computation.17 | convolution fusion | flops 604504064 | bytes 14155776 | tf_op jit(solution)/shard_map/fcq,fqs->fcs/dot_general | solution.py:54
  143.9 0.0 all-reduce.5.cloned.1.call-update
  144.0 57.5 %all-reduce.5.cloned.1.call-done = bf16[16,32,1024]{2,1,0:T(8,128)(2,1)} async-done(((bf16[16,32,1024]{2,1,0:T(8,128)(2,1)}), bf16[16,32,1024]{2,1,0:T(8,128)(2,1)}) %all-reduce.5.cloned.1.call-update) | async-done | bytes 1048592 | tf_op jit(solution)/shard_map/psum | solution.py:57
  201.5 8.8 %convolution_convert_fusion.4 = bf16[16,32,512]{2,1,0:T(8,128)(2,1)S(1)} fusion(bf16[16,32,1024]{2,1,0:T(8,128)(2,1)} %all-reduce.5.cloned.1.call-done, f32[16,1024]{1,0:T(8,128)S(1)} %copy-done.4, f32[16,1024]{1,0:T(8,128)S(1)} %pad_maximum_fusion, bf16[16,256,512]{2,1,0:T(8,128)(2,1)} %get-tuple-element.7, bf16[16,256,512]{2,1,0:T(8,128)(2,1)} %fusion.20, ...), kind=kOutput, calls=%fused_computation.19 | convolution fusion | flops 606339072 | bytes 14286848 | tf_op jit(solution)/shard_map/fcs,fqs->fcq/dot_general | solution.py:59
  210.3 0.1 copy.91
  210.4 0.3 copy.70
  210.7 10.8 %all_to_all.62 = bf16[32,256,32]{1,2,0:T(8,128)(2,1)S(1)} all-to-all(bf16[32,256,32]{1,2,0:T(8,128)(2,1)S(1)} %copy.70), channel_id=1, replica_groups=mesh['freq'=4,'param'=8] {'freq'}, dimensions={0} | all-to-all | bytes 1048576 | tf_op jit(solution)/shard_map/all_to_all | solution.py:67
  221.5 9.7 %fusion.2 = (f32[8,256,512]{2,1,0:T(8,128)}, f32[8,256,512]{2,1,0:T(8,128)}) fusion(f32[2,8,256,512]{3,2,1,0:T(8,128)} %param.9, f32[8,256,512]{2,1,0:T(8,128)} %get-tuple-element.5, f32[8]{0:T(128)S(1)} %copy-done.3, f32[8,256,512]{2,1,0:T(8,128)S(1)} %copy-done.1, f32[8,256,512]{2,1,0:T(8,128)} %get-tuple-element.10, f32[8,256,512]{2,1,0:T(8,128)} %param.8, ...), kind=kOutput, calls=%fused_computation.6 | convolution fusion | flops 286261248 | bytes 30015520 | tf_op jit(solution)/shard_map/dot_general | solution.py:68
  (16 shorter events, 0.2 us)
Async XLA Ops:
  12.2 15.5 %all-to-all-start = ((bf16[8,256,128]{1,0,2:T(8,128)(2,1)}), bf16[8,256,128]{1,0,2:T(8,128)(2,1)S(1)}, u32[]{:S(2)}, u32[]{:S(2)}) async-start(bf16[8,256,128]{1,0,2:T(8,128)(2,1)} %bitcast.48), calls=%async_computation | async-start | bytes 1048576 | tf_op jit(solution)/shard_map/all_to_all | solution.py:48
  17.4 80.1 %all-reduce.3.cloned.1.call-start = ((), (), s32[]{:S(2)}) async-start(), calls=%async_computation.4 | async-start | bytes 2097152 | tf_op jit(solution)/shard_map/psum | solution.py:57
  27.8 8.5 %copy-start.2 = (f32[16,512]{1,0:T(8,128)S(1)}, f32[16,512]{1,0:T(8,128)}, u32[]{:S(2)}) copy-start(f32[16,512]{1,0:T(8,128)} %param.12) | copy-start | bytes 98308
  27.8 69.7 %copy-start.4 = (f32[16,1024]{1,0:T(8,128)S(1)}, f32[16,1024]{1,0:T(8,128)}, u32[]{:S(2)}) copy-start(f32[16,1024]{1,0:T(8,128)} %param.11) | copy-start | bytes 196612
  36.3 165.2 %all-reduce.5.cloned.1.call-start = ((), (), s32[]{:S(2)}) async-start(), calls=%async_computation.5 | async-start | bytes 2097152 | tf_op jit(solution)/shard_map/psum | solution.py:57
  106.2 11.2 %copy-start = (f32[8,256,512]{2,1,0:T(8,128)S(1)}, f32[8,256,512]{2,1,0:T(8,128)}, u32[]{:S(2)}) copy-start(f32[8,256,512]{2,1,0:T(8,128)} %param.7) | copy-start | bytes 12582916
  106.2 11.2 %copy-start.3 = (f32[8]{0:T(128)S(1)}, f32[8]{0:T(128)}, u32[]{:S(2)}) copy-start(f32[8]{0:T(128)} %param.13) | copy-start | bytes 100
  210.3 11.2 %copy-start.1 = (f32[8,256,512]{2,1,0:T(8,128)S(1)}, f32[8,256,512]{2,1,0:T(8,128)}, u32[]{:S(2)}) copy-start(f32[8,256,512]{2,1,0:T(8,128)} %param.7) | copy-start | bytes 12582916
Sparse Core Ops, SparseCore 0:
  36.4 61.0 all-reduce.2
  144.1 57.3 all-reduce.4
where the time goes:
time: 238 us
  waiting for transfers between devices  119 us (50%)
  matrix products  53.1 us (22%)
  blocking collectives  31.1 us (13%)
  between operations  14.2 us (6%)
  local copies, waits for them, and re-layouts  8.32 us (3%)
  other arithmetic  7.49 us (3%)
  starting transfers between devices  5.23 us (2%)
    psum x2, waiting for transfers between devices, on_device(): lax.psum(partial_data.astype(jnp.bfloat16), 'param').astype(jnp.float32)  119 us
    all_to_all x2, blocking collectives, on_device(): lax.all_to_all(adjoint, 'freq', split_axis=0, concat_axis=2, tiled=True)  21.6 us
    dot_general x2, matrix products, on_device(): jnp.einsum('fcs,fqs->fcq', weighted, kernel, preferred_element_type=jnp.f...  17.6 us
    dot_general x2, matrix products, on_device(): jnp.dot(own_adjoint.reshape(chains_loc * slab_rows, 2 * freq_total), inve...  17.1 us
    dot_general x2, matrix products, on_device(): jnp.einsum('fcq,fqs->fcs', mixed_spec, kernel, preferred_element_type=jnp...  16.9 us
    all_to_all x1, blocking collectives, on_device(): lax.all_to_all(local_spec, 'freq', split_axis=2, concat_axis=0, tiled=True)  9.53 us
    squeeze x1, local copies, waits for them, and re-layouts, on_device(): green_im = green[1]  5.93 us
    all_to_all x1, starting transfers between devices, on_device(): lax.all_to_all(local_spec, 'freq', split_axis=2, concat_axis=0, tiled=True)  5.19 us
  transfers between devices with their start and end apart: 3, of which 2 were waited for; matrix products, arithmetic and copies ran while one was open for 4% of the time, Pallas kernels for 0%

commit v1 on v0

--- a/solution.py
+++ b/solution.py
@@ -6,6 +6,11 @@
 
 decay_rate = 0.9
 step_length = 0.5
+
+
+def summed_here(shard, mesh_axis):
+    parts = lax.all_gather(shard, mesh_axis)
+    return jnp.sum(parts, axis=0)
 
 
 def spectral_table(time_len, freq_total):
@@ -54,7 +59,7 @@
         partial_data = jnp.einsum(
             "fcq,fqs->fcs", mixed_spec, kernel, preferred_element_type=jnp.float32
         )
-        predicted = lax.psum(partial_data.astype(jnp.bfloat16), "param").astype(jnp.float32)
+        predicted = summed_here(partial_data.astype(jnp.bfloat16), "param").astype(jnp.float32)
         weighted = (weights[:, None, :] * (predicted - observed[:, None, :])).astype(jnp.bfloat16)
         adjoint = jnp.einsum(
             "fcs,fqs->fcq", weighted, kernel, preferred_element_type=jnp.float32

time: 238 us -> 298 us (1.25)
  waiting for transfers between devices: 119 us -> 163 us
  other arithmetic: 7.49 us -> 18.6 us
  blocking collectives: 31.1 us -> 35.4 us
    all_gather x0 -> x2, waiting for transfers between devices: none -> 163 us  [summed_here(): parts = lax.all_gather(shard, mesh_axis)]
    psum x2 -> x0, waiting for transfers between devices: 119 us -> none  [on_device(): lax.psum(partial_data.astype(jnp.bfloat16), 'param').astype(jnp.float32)]
    reduce_sum x0 -> x2, other arithmetic: none -> 11.1 us  [summed_here(): return jnp.sum(parts, axis=0)]
    all_to_all x2, blocking collectives: 21.6 us -> 25.3 us  [on_device(): lax.all_to_all(adjoint, 'freq', split_axis=0, concat_axis=2, tiled=True)]
  transfers between devices with their start and end apart: 3 -> 3, of which waited for: 2 -> 2; matrix products, arithmetic and copies ran while one was open for 4% -> 3% of each run, Pallas kernels for 0% -> 0%
where the time goes in v1:
time: 298 us; the launch traced here: 297 us
  waiting for transfers between devices  163 us (55%)
  matrix products  52.3 us (18%)
  blocking collectives  35.4 us (12%)
  other arithmetic  18.6 us (6%)
  between operations  14.3 us (5%)
  local copies, waits for them, and re-layouts  8.31 us (3%)
  starting transfers between devices  5.23 us (2%)
    all_gather x2, waiting for transfers between devices, summed_here(): parts = lax.all_gather(shard, mesh_axis)  163 us
    all_to_all x2, blocking collectives, on_device(): lax.all_to_all(adjoint, 'freq', split_axis=0, concat_axis=2, tiled=True)  25.3 us
    dot_general x2, matrix products, on_device(): jnp.einsum('fcs,fqs->fcq', weighted, kernel, preferred_element_type=jnp.f...  17.2 us
    dot_general x2, matrix products, on_device(): jnp.dot(own_adjoint.reshape(chains_loc * slab_rows, 2 * freq_total), inve...  17 us
    dot_general x2, matrix products, on_device(): jnp.einsum('fcq,fqs->fcs', mixed_spec, kernel, preferred_element_type=jnp...  16.6 us
    reduce_sum x2, other arithmetic, summed_here(): return jnp.sum(parts, axis=0)  11.1 us
    all_to_all x1, blocking collectives, on_device(): lax.all_to_all(local_spec, 'freq', split_axis=2, concat_axis=0, tiled=True)  10.1 us
  transfers between devices with their start and end apart: 3, of which 2 were waited for; matrix products, arithmetic and copies ran while one was open for 3% of the time, Pallas kernels for 0%

profile of v1, /device:TPU:0, one launch (start us, length us, event | category | flops | bytes accessed | tf_op | source)
XLA Modules:
  0.0 297.2 jit_solution(3764874065682101320)
XLA Ops:
  7.2 0.6 fusion.19
  7.8 0.1 copy.56
  7.9 0.1 convert_element_type.85
  8.0 2.5 convert_element_type.86
  10.5 0.8 convolution_convert_fusion.1
  11.3 0.9 copy.86
  12.2 5.2 %all-to-all-start = ((bf16[8,256,128]{1,0,2:T(8,128)(2,1)}), bf16[8,256,128]{1,0,2:T(8,128)(2,1)S(1)}, u32[]{:S(2)}, u32[]{:S(2)}) async-start(bf16[8,256,128]{1,0,2:T(8,128)(2,1)} %bitcast.50), calls=%async_computation | async-start | bytes 1048576 | tf_op jit(solution)/shard_map/all_to_all | solution.py:53
  17.4 5.9 %slice_bitcast_fusion = (bf16[16,256,512]{2,1,0:T(8,128)(2,1)}, bf16[16,256,512]{2,1,0:T(8,128)(2,1)}) fusion(bf16[2,16,256,512]{3,2,1,0:T(8,128)(2,1)} %param.10), kind=kLoop, calls=%fused_computation.11 | loop fusion | bytes 16777216 | tf_op jit(solution)/shard_map/squeeze | solution.py:37
  23.3 4.4 %fusion.20 = bf16[16,256,512]{2,1,0:T(8,128)(2,1)} fusion(bf16[2,16,256,512]{3,2,1,0:T(8,128)(2,1)} %param.10), kind=kLoop, calls=%fused_computation.46 | loop fusion | flops 2097152 | bytes 8388608 | tf_op jit(solution)/shard_map/neg | solution.py:39
  27.8 0.0 copy-start.2
  27.8 8.3 %convolution_convert_fusion.3 = bf16[16,32,1024]{2,1,0:T(8,128)(2,1)} fusion(bf16[16,32,512]{2,1,0:T(8,128)(2,1)S(1)} %bitcast.102, bf16[16,256,512]{2,1,0:T(8,128)(2,1)} %get-tuple-element.7, bf16[16,256,512]{2,1,0:T(8,128)(2,1)} %fusion.20, bf16[16,256,512]{2,1,0:T(8,128)(2,1)} %get-tuple-element.6), kind=kOutput, calls=%fused_computation.18 | convolution fusion | flops 604504064 | bytes 14155776 | tf_op jit(solution)/shard_map/fcq,fqs->fcs/dot_general | solution.py:59
  36.1 0.0 all-gather.5.cloned.1.call-update
  36.2 0.0 all-gather.7.cloned.1.call-start
  36.2 83.9 %all-gather.5.cloned.1.call-done = bf16[128,32,1024]{2,1,0:T(8,128)(2,1)} async-done(((bf16[16,32,1024]{2,1,0:T(8,128)(2,1)}), bf16[128,32,1024]{2,1,0:T(8,128)(2,1)}) %all-gather.5.cloned.1.call-update) | async-done | bytes 8388624 | tf_op jit(solution)/shard_map/all_gather | solution.py:12
  120.1 5.6 %reduce_sum.24 = bf16[16,32,1024]{2,1,0:T(8,128)(2,1)S(1)} reduce(bf16[8,16,32,1024]{3,2,1,0:T(8,128)(2,1)} %bitcast.89, bf16[]{:T(256)} %constant.29.clone.1), dimensions={0}, to_apply=%region_0.1 | reduce | flops 3670016 | bytes 9437186 | tf_op jit(solution)/shard_map/reduce_sum | solution.py:13
  125.7 8.6 %convolution_convert_fusion.5 = bf16[16,32,512]{2,1,0:T(8,128)(2,1)S(1)} fusion(bf16[16,32,1024]{2,1,0:T(8,128)(2,1)S(1)} %reduce_sum.24, f32[16,1024]{1,0:T(8,128)S(1)} %copy-done.4, f32[16,1024]{1,0:T(8,128)S(1)} %pad_maximum_fusion, bf16[16,256,512]{2,1,0:T(8,128)(2,1)} %get-tuple-element.7, bf16[16,256,512]{2,1,0:T(8,128)(2,1)} %fusion.20, ...), kind=kOutput, calls=%fused_computation.20 | convolution fusion | flops 606339072 | bytes 14286848 | tf_op jit(solution)/shard_map/fcs,fqs->fcq/dot_general | solution.py:64
  134.3 0.1 copy.92
  134.4 0.3 copy.61
  134.7 12.6 %all_to_all.60 = bf16[32,256,32]{1,2,0:T(8,128)(2,1)S(1)} all-to-all(bf16[32,256,32]{1,2,0:T(8,128)(2,1)S(1)} %copy.61), channel_id=1, replica_groups=mesh['freq'=4,'param'=8] {'freq'}, dimensions={0} | all-to-all | bytes 1048576 | tf_op jit(solution)/shard_map/all_to_all | solution.py:72
  147.4 7.3 %fusion.22 = (bf16[8,256,512]{2,1,0:T(8,128)(2,1)S(1)}, f32[8,256,512]{2,1,0:T(8,128)}, f32[8,256,512]{2,1,0:T(8,128)}) fusion(f32[2,8,256,512]{3,2,1,0:T(8,128)} %param.9, f32[8,256,512]{2,1,0:T(8,128)S(1)} %copy-done, f32[8]{0:T(128)S(1)} %copy-done.3, f32[8,256,512]{2,1,0:T(8,128)} %param.8, bf16[8,256,128]{1,2,0:T(8,128)(2,1)S(1)} %bitcast.92, ...), kind=kOutput, calls=%fused_computation.47 | convolution fusion | flops 281018368 | bytes 23724064 | tf_op jit(solution)/shard_map/dot_general | solution.py:73
  154.6 0.7 convolution_convert_fusion
  155.3 0.4 copy.65
  155.7 10.1 %all_to_all.61 = bf16[8,256,128]{1,0,2:T(8,128)(2,1)S(1)} all-to-all(bf16[8,256,128]{1,0,2:T(8,128)(2,1)S(1)} %copy.65), channel_id=1, replica_groups=mesh['freq'=4,'param'=8] {'freq'}, dimensions={2} | all-to-all | bytes 1048576 | tf_op jit(solution)/shard_map/all_to_all | solution.py:53
  165.9 8.3 %convolution_convert_fusion.2 = bf16[16,32,1024]{2,1,0:T(8,128)(2,1)} fusion(bf16[16,32,512]{2,1,0:T(8,128)(2,1)S(1)} %bitcast.104, bf16[16,256,512]{2,1,0:T(8,128)(2,1)} %get-tuple-element.7, bf16[16,256,512]{2,1,0:T(8,128)(2,1)} %fusion.20, bf16[16,256,512]{2,1,0:T(8,128)(2,1)} %get-tuple-element.6), kind=kOutput, calls=%fused_computation.17 | convolution fusion | flops 604504064 | bytes 14155776 | tf_op jit(solution)/shard_map/fcq,fqs->fcs/dot_general | solution.py:59
  174.2 0.0 all-gather.7.cloned.1.call-update
  174.2 79.2 %all-gather.7.cloned.1.call-done = bf16[128,32,1024]{2,1,0:T(8,128)(2,1)} async-done(((bf16[16,32,1024]{2,1,0:T(8,128)(2,1)}), bf16[128,32,1024]{2,1,0:T(8,128)(2,1)}) %all-gather.7.cloned.1.call-update) | async-done | bytes 8388624 | tf_op jit(solution)/shard_map/all_gather | solution.py:12
  253.4 5.5 %reduce_sum.25 = bf16[16,32,1024]{2,1,0:T(8,128)(2,1)S(1)} reduce(bf16[8,16,32,1024]{3,2,1,0:T(8,128)(2,1)} %bitcast.90, bf16[]{:T(256)} %constant.29.clone.1), dimensions={0}, to_apply=%region_1.2 | reduce | flops 3670016 | bytes 9437186 | tf_op jit(solution)/shard_map/reduce_sum | solution.py:13
  259.0 8.6 %convolution_convert_fusion.4 = bf16[16,32,512]{2,1,0:T(8,128)(2,1)S(1)} fusion(bf16[16,32,1024]{2,1,0:T(8,128)(2,1)S(1)} %reduce_sum.25, f32[16,1024]{1,0:T(8,128)S(1)} %copy-done.4, f32[16,1024]{1,0:T(8,128)S(1)} %pad_maximum_fusion, bf16[16,256,512]{2,1,0:T(8,128)(2,1)} %get-tuple-element.7, bf16[16,256,512]{2,1,0:T(8,128)(2,1)} %fusion.20, ...), kind=kOutput, calls=%fused_computation.19 | convolution fusion | flops 606339072 | bytes 14286848 | tf_op jit(solution)/shard_map/fcs,fqs->fcq/dot_general | solution.py:64
  267.6 0.1 copy.91
  267.7 0.3 copy.70
  268.0 12.6 %all_to_all.62 = bf16[32,256,32]{1,2,0:T(8,128)(2,1)S(1)} all-to-all(bf16[32,256,32]{1,2,0:T(8,128)(2,1)S(1)} %copy.70), channel_id=1, replica_groups=mesh['freq'=4,'param'=8] {'freq'}, dimensions={0} | all-to-all | bytes 1048576 | tf_op jit(solution)/shard_map/all_to_all | solution.py:72
  280.6 9.7 %fusion.2 = (f32[8,256,512]{2,1,0:T(8,128)}, f32[8,256,512]{2,1,0:T(8,128)}) fusion(f32[2,8,256,512]{3,2,1,0:T(8,128)} %param.9, f32[8,256,512]{2,1,0:T(8,128)} %get-tuple-element.5, f32[8]{0:T(128)S(1)} %copy-done.3, f32[8,256,512]{2,1,0:T(8,128)S(1)} %copy-done.1, f32[8,256,512]{2,1,0:T(8,128)} %get-tuple-element.10, f32[8,256,512]{2,1,0:T(8,128)} %param.8, ...), kind=kOutput, calls=%fused_computation.6 | convolution fusion | flops 286261248 | bytes 30015520 | tf_op jit(solution)/shard_map/dot_general | solution.py:73
  (18 shorter events, 0.2 us)
Async XLA Ops:
  12.2 15.5 %all-to-all-start = ((bf16[8,256,128]{1,0,2:T(8,128)(2,1)}), bf16[8,256,128]{1,0,2:T(8,128)(2,1)S(1)}, u32[]{:S(2)}, u32[]{:S(2)}) async-start(bf16[8,256,128]{1,0,2:T(8,128)(2,1)} %bitcast.50), calls=%async_computation | async-start | bytes 1048576 | tf_op jit(solution)/shard_map/all_to_all | solution.py:53
  17.4 102.7 %all-gather.5.cloned.1.call-start = ((), (), s32[]{:S(2)}) async-start(), calls=%async_computation.4 | async-start | bytes 9437184 | tf_op jit(solution)/shard_map/all_gather | solution.py:12
  27.8 8.4 %copy-start.2 = (f32[16,512]{1,0:T(8,128)S(1)}, f32[16,512]{1,0:T(8,128)}, u32[]{:S(2)}) copy-start(f32[16,512]{1,0:T(8,128)} %param.12) | copy-start | bytes 98308
  36.2 217.3 %all-gather.7.cloned.1.call-start = ((), (), s32[]{:S(2)}) async-start(), calls=%async_computation.5 | async-start | bytes 9437184 | tf_op jit(solution)/shard_map/all_gather | solution.py:12
  120.1 5.6 %copy-start.4 = (f32[16,1024]{1,0:T(8,128)S(1)}, f32[16,1024]{1,0:T(8,128)}, u32[]{:S(2)}) copy-start(f32[16,1024]{1,0:T(8,128)} %param.11) | copy-start | bytes 196612
  134.3 13.1 %copy-start = (f32[8,256,512]{2,1,0:T(8,128)S(1)}, f32[8,256,512]{2,1,0:T(8,128)}, u32[]{:S(2)}) copy-start(f32[8,256,512]{2,1,0:T(8,128)} %param.7) | copy-start | bytes 12582916
  134.3 13.1 %copy-start.3 = (f32[8]{0:T(128)S(1)}, f32[8]{0:T(128)}, u32[]{:S(2)}) copy-start(f32[8]{0:T(128)} %param.13) | copy-start | bytes 100
  267.6 13.1 %copy-start.1 = (f32[8,256,512]{2,1,0:T(8,128)S(1)}, f32[8,256,512]{2,1,0:T(8,128)}, u32[]{:S(2)}) copy-start(f32[8,256,512]{2,1,0:T(8,128)} %param.7) | copy-start | bytes 12582916
Sparse Core Ops, SparseCore 0:
  36.3 83.7 all-gather.4
  174.3 79.0 all-gather.6
